TPU v7x, 32 devices: a whole 2x2x4 slice. The times are simulated.
32 devices in a mesh: wide: 8 (over y, x, core), narrow: 4 (over z).
Axes of the slice: x: 2, y: 2, z: 4, core: 2. Of those that a mesh axis runs over, the one named last changes fastest.
Arguments:
- hidden_in: bfloat16 [16, 1024, 768], P('wide', 'narrow'), may hold values from -6 to 6
- positions: int32 [16, 1024], P('wide', 'narrow'), may hold values from 0 to 1023, as said below
- time_index: int32 [16], P('wide'), may hold values from 0 to 1023
- cond_table: bfloat16 [1024, 128], replicated, may hold values from -5 to 5
- ada_weight: bfloat16 [128, 4608], replicated, may hold values from -0.5 to 0.5
- norm1_gain: bfloat16 [768], replicated, may hold values from 0.099609375 to 1.8984375
- qkv_weight: bfloat16 [768, 2304], replicated, may hold values from -0.21875 to 0.21875
- out_weight: bfloat16 [768, 768], replicated, may hold values from -0.875 to 0.875
- norm2_gain: bfloat16 [768], replicated, may hold values from 0.099609375 to 1.8984375
- up_weight: bfloat16 [768, 3072], replicated, may hold values from -0.21875 to 0.21875
- down_weight: bfloat16 [3072, 768], replicated, may hold values from -0.21875 to 0.21875
- cotangent: bfloat16 [16, 1024, 768], P('wide', 'narrow'), may hold values from -6 to 6
Outputs:
- hidden_out: bfloat16 [16, 1024, 768], P('wide', 'narrow')
- hidden_grad: bfloat16 [16, 1024, 768], P('wide', 'narrow')
- cond_table_grad: float32 [1024, 128], P('wide', 'narrow')
- ada_weight_grad: float32 [128, 4608], P('narrow', 'wide')
- norm1_gain_grad: float32 [768], P('wide')
- qkv_weight_grad: float32 [768, 2304], P('wide', 'narrow')
- out_weight_grad: float32 [768, 768], P('wide', 'narrow')
- norm2_gain_grad: float32 [768], P('wide')
- up_weight_grad: float32 [768, 3072], P('wide', 'narrow')
- down_weight_grad: float32 [3072, 768], P('wide', 'narrow')
Inputs may be any that keep to these rules, and one draw needn't show every extreme that they name: positions count up by one from the start of each packed document, every row starts a document at its first token, and one row is a single document.
All inputs are finite; a program needn't handle non-finite values.
Results may differ from a plain program's by a relative error of at most 0.015.
The roundings to bfloat16 on the way count: a program that leaves them out, or rounds other values in their place, can miss the bound.
Values may be sent and summed in bfloat16 or wider, within the bound.
No kernel may reach another device: no remote copies, remote signals or barrier semaphores. Data moves between devices by JAX's collectives and lax.ppermute only.
A program may use at most 192 MiB of HBM per device.

v0:
```python
import jax
import jax.numpy as jnp
from jax import lax
from jax.sharding import PartitionSpec as P

HEAD_DIM = 64


HIGHEST = lax.Precision.HIGHEST
norm_eps = 1e-05


def norm_mod(hidden, gain, shift, scale):
    center = hidden - jnp.mean(hidden, axis=-1, keepdims=True)
    variance = jnp.mean(center * center, axis=-1, keepdims=True)
    return center * lax.rsqrt(variance + norm_eps) * gain * (1.0 + scale) + shift


def rotary(values, positions):
    half_dim = values.shape[-1] // 2
    frequency = 10000.0 ** (-jnp.arange(half_dim, dtype=jnp.float32) / half_dim)
    angles = positions.astype(jnp.float32)[..., None, None] * frequency
    cosine = jnp.cos(angles)
    sine = jnp.sin(angles)
    first_half = values[..., :half_dim]
    second_half = values[..., half_dim:]
    return jnp.concatenate(
        [first_half * cosine - second_half * sine, second_half * cosine + first_half * sine],
        axis=-1,
    )


def gelu_tanh(values):
    return jax.nn.gelu(values, approximate=True)


def tdot(left, right):
    return lax.dot_general(
        left, right, (((0,), (0,)), ((), ())), preferred_element_type=jnp.float32
    )


def ndot(left, right):
    return lax.dot_general(
        left, right, (((1,), (1,)), ((), ())), preferred_element_type=jnp.float32
    )


def attend(row_item):
    queries, key_rows, value_rows = row_item
    length = queries.shape[0]
    local_heads = queries.shape[1] // HEAD_DIM
    queries = queries.reshape(length, local_heads, HEAD_DIM)
    key_rows = key_rows.reshape(length, local_heads, HEAD_DIM)
    value_rows = value_rows.reshape(length, local_heads, HEAD_DIM)
    scores = jnp.einsum(
        "qhd,khd->hqk", queries, key_rows, preferred_element_type=jnp.float32
    ) * HEAD_DIM ** (-0.5)
    row_max = jnp.max(scores, axis=-1, keepdims=True)
    expo = jnp.exp(scores - row_max)
    row_total = jnp.sum(expo, axis=-1, keepdims=True)
    probs = expo / row_total
    log_total = row_max + jnp.log(row_total)
    result = jnp.einsum(
        "hqk,khd->qhd", probs.astype(jnp.bfloat16), value_rows, preferred_element_type=jnp.float32
    )
    return (result.astype(jnp.bfloat16).reshape(length, local_heads * HEAD_DIM), log_total)


def attend_back(row_item):
    queries, key_rows, value_rows, d_result, log_total = row_item
    length = queries.shape[0]
    local_heads = queries.shape[1] // HEAD_DIM
    queries = queries.reshape(length, local_heads, HEAD_DIM)
    key_rows = key_rows.reshape(length, local_heads, HEAD_DIM)
    value_rows = value_rows.reshape(length, local_heads, HEAD_DIM)
    d_result = d_result.reshape(length, local_heads, HEAD_DIM)
    score_scale = HEAD_DIM ** (-0.5)
    scores = (
        jnp.einsum("qhd,khd->hqk", queries, key_rows, preferred_element_type=jnp.float32)
        * score_scale
    )
    probs = jnp.exp(scores - log_total)
    d_values = jnp.einsum(
        "hqk,qhd->khd", probs.astype(jnp.bfloat16), d_result, preferred_element_type=jnp.float32
    )
    d_probs = jnp.einsum("qhd,khd->hqk", d_result, value_rows, preferred_element_type=jnp.float32)
    d_scores = probs * (d_probs - jnp.sum(probs * d_probs, axis=-1, keepdims=True))
    d_low = d_scores.astype(jnp.bfloat16)
    d_queries = (
        jnp.einsum("hqk,khd->qhd", d_low, key_rows, preferred_element_type=jnp.float32)
        * score_scale
    )
    d_keys = (
        jnp.einsum("hqk,qhd->khd", d_low, queries, preferred_element_type=jnp.float32) * score_scale
    )
    width_local = local_heads * HEAD_DIM
    return (
        d_queries.astype(jnp.bfloat16).reshape(length, width_local),
        d_keys.astype(jnp.bfloat16).reshape(length, width_local),
        d_values.astype(jnp.bfloat16).reshape(length, width_local),
    )


def blocks_rows_wide(grad, wide_count, narrow_count):
    rows, cols = grad.shape
    split = grad.reshape(wide_count, rows // wide_count, narrow_count, cols // narrow_count)
    return split.transpose(0, 2, 1, 3).reshape(wide_count, narrow_count, -1)


def blocks_rows_narrow(grad, wide_count, narrow_count):
    rows, cols = grad.shape
    split = grad.reshape(narrow_count, rows // narrow_count, wide_count, cols // wide_count)
    return split.transpose(2, 0, 1, 3).reshape(wide_count, narrow_count, -1)


def blocks_gain(grad, wide_count, narrow_count):
    split = grad.reshape(wide_count, 1, grad.shape[0] // wide_count)
    return jnp.broadcast_to(split, (wide_count, narrow_count, grad.shape[0] // wide_count))


def on_device(
    hidden_in,
    positions,
    time_index,
    cond_table,
    ada_weight,
    norm1_gain,
    qkv_weight,
    out_weight,
    norm2_gain,
    up_weight,
    down_weight,
    cotangent,
):
    row_count, part_len, model_width = hidden_in.shape
    tokens = row_count * part_len
    heads_all = model_width // HEAD_DIM
    times = cond_table.shape[0]
    onehot = (time_index[:, None] == jnp.arange(times, dtype=jnp.int32)[None, :]).astype(
        jnp.float32
    )
    embedded = jnp.dot(
        onehot,
        cond_table.astype(jnp.float32),
        precision=HIGHEST,
        preferred_element_type=jnp.float32,
    )
    condition_low = jax.nn.silu(embedded).astype(jnp.bfloat16)
    modulation = jnp.dot(condition_low, ada_weight, preferred_element_type=jnp.float32)
    pieces = [
        modulation[:, None, index * model_width : (index + 1) * model_width] for index in range(6)
    ]
    shift_one, scale_one, gate_one, shift_two, scale_two, gate_two = pieces
    hidden_full = hidden_in.astype(jnp.float32)
    gain_one = norm1_gain.astype(jnp.float32)
    gain_two = norm2_gain.astype(jnp.float32)
    norm_one = (
        norm_mod(hidden_full, gain_one, shift_one, scale_one)
        .astype(jnp.bfloat16)
        .reshape(tokens, model_width)
    )
    qkv = jnp.dot(norm_one, qkv_weight, preferred_element_type=jnp.float32).reshape(
        row_count, part_len, 3, heads_all, HEAD_DIM
    )
    query_pre = qkv[:, :, 0]
    key_pre = qkv[:, :, 1]
    query_low = (
        rotary(query_pre, positions).astype(jnp.bfloat16).reshape(row_count, part_len, model_width)
    )
    key_low = (
        rotary(key_pre, positions).astype(jnp.bfloat16).reshape(row_count, part_len, model_width)
    )
    value_low = qkv[:, :, 2].astype(jnp.bfloat16).reshape(row_count, part_len, model_width)
    query_heads, key_heads, value_heads = (
        lax.all_to_all(query_low, "narrow", split_axis=2, concat_axis=1, tiled=True),
        lax.all_to_all(key_low, "narrow", split_axis=2, concat_axis=1, tiled=True),
        lax.all_to_all(value_low, "narrow", split_axis=2, concat_axis=1, tiled=True),
    )
    attended_heads, log_totals = lax.map(attend, (query_heads, key_heads, value_heads))
    attended = lax.all_to_all(
        attended_heads, "narrow", split_axis=1, concat_axis=2, tiled=True
    ).reshape(tokens, model_width)
    projected = jnp.dot(attended, out_weight, preferred_element_type=jnp.float32).reshape(
        row_count, part_len, model_width
    )
    middle = hidden_full + gate_one * projected
    norm_two = (
        norm_mod(middle, gain_two, shift_two, scale_two)
        .astype(jnp.bfloat16)
        .reshape(tokens, model_width)
    )
    up_part = jnp.dot(norm_two, up_weight, preferred_element_type=jnp.float32)
    activated = gelu_tanh(up_part).astype(jnp.bfloat16)
    down_part = jnp.dot(activated, down_weight, preferred_element_type=jnp.float32).reshape(
        row_count, part_len, model_width
    )
    hidden_out = (middle + gate_two * down_part).astype(jnp.bfloat16)
    d_out = cotangent.astype(jnp.float32)
    d_gate_two = jnp.sum(d_out * down_part, axis=1)
    d_down = (d_out * gate_two).astype(jnp.bfloat16).reshape(tokens, model_width)
    grad_down = tdot(activated, d_down)
    d_activated = ndot(d_down, down_weight)
    unused_gelu, gelu_back = jax.vjp(gelu_tanh, up_part)
    d_up = gelu_back(d_activated)[0].astype(jnp.bfloat16)
    grad_up = tdot(norm_two, d_up)
    d_norm_two = ndot(d_up, up_weight).reshape(row_count, part_len, model_width)
    unused_two, norm_two_back = jax.vjp(norm_mod, middle, gain_two, shift_two, scale_two)
    d_middle_norm, grad_gain_two, d_shift_two, d_scale_two = norm_two_back(d_norm_two)
    d_middle = d_out + d_middle_norm
    d_gate_one = jnp.sum(d_middle * projected, axis=1)
    d_projected = (d_middle * gate_one).astype(jnp.bfloat16).reshape(tokens, model_width)
    grad_out = tdot(attended, d_projected)
    d_attended = (
        ndot(d_projected, out_weight).astype(jnp.bfloat16).reshape(row_count, part_len, model_width)
    )
    d_attended_heads = lax.all_to_all(d_attended, "narrow", split_axis=2, concat_axis=1, tiled=True)
    d_query_heads, d_key_heads, d_value_heads = lax.map(
        attend_back, (query_heads, key_heads, value_heads, d_attended_heads, log_totals)
    )
    d_query, d_key, d_value = (
        lax.all_to_all(d_query_heads, "narrow", split_axis=1, concat_axis=2, tiled=True),
        lax.all_to_all(d_key_heads, "narrow", split_axis=1, concat_axis=2, tiled=True),
        lax.all_to_all(d_value_heads, "narrow", split_axis=1, concat_axis=2, tiled=True),
    )

    def rotate_both(query_part, key_part):
        return (rotary(query_part, positions), rotary(key_part, positions))

    unused_rot, rotate_back = jax.vjp(rotate_both, query_pre, key_pre)
    head_shape = (row_count, part_len, heads_all, HEAD_DIM)
    d_query_pre, d_key_pre = rotate_back(
        (
            d_query.astype(jnp.float32).reshape(head_shape),
            d_key.astype(jnp.float32).reshape(head_shape),
        )
    )
    d_qkv = jnp.stack(
        [d_query_pre, d_key_pre, d_value.astype(jnp.float32).reshape(head_shape)], axis=2
    )
    d_qkv = d_qkv.astype(jnp.bfloat16).reshape(tokens, 3 * model_width)
    grad_qkv = tdot(norm_one, d_qkv)
    d_norm_one = ndot(d_qkv, qkv_weight).reshape(row_count, part_len, model_width)
    unused_one, norm_one_back = jax.vjp(norm_mod, hidden_full, gain_one, shift_one, scale_one)
    d_hidden_norm, grad_gain_one, d_shift_one, d_scale_one = norm_one_back(d_norm_one)
    hidden_grad = (d_middle + d_hidden_norm).astype(jnp.bfloat16)
    d_modulation = jnp.concatenate(
        [
            d_shift_one.reshape(row_count, model_width),
            d_scale_one.reshape(row_count, model_width),
            d_gate_one,
            d_shift_two.reshape(row_count, model_width),
            d_scale_two.reshape(row_count, model_width),
            d_gate_two,
        ],
        axis=1,
    )
    grad_ada = lax.dot_general(
        condition_low.astype(jnp.float32),
        d_modulation,
        (((0,), (0,)), ((), ())),
        precision=HIGHEST,
        preferred_element_type=jnp.float32,
    )
    d_condition = lax.dot_general(
        d_modulation,
        ada_weight.astype(jnp.float32),
        (((1,), (1,)), ((), ())),
        precision=HIGHEST,
        preferred_element_type=jnp.float32,
    )
    unused_silu, silu_back = jax.vjp(jax.nn.silu, embedded)
    d_embedded = silu_back(d_condition)[0]
    grad_table = lax.dot_general(
        onehot,
        d_embedded,
        (((0,), (0,)), ((), ())),
        precision=HIGHEST,
        preferred_element_type=jnp.float32,
    )
    wide_count = lax.axis_size("wide")
    narrow_count = lax.axis_size("narrow")
    weight_grads = [
        grad_table,
        grad_ada,
        grad_gain_one,
        grad_qkv,
        grad_out,
        grad_gain_two,
        grad_up,
        grad_down,
    ]
    kinds = ["wide", "narrow", "gain", "wide", "wide", "gain", "wide", "wide"]
    block_list = []
    local_shapes = []
    for item, kind in zip(weight_grads, kinds):
        if kind == "wide":
            block_list.append(blocks_rows_wide(item, wide_count, narrow_count))
            local_shapes.append((item.shape[0] // wide_count, item.shape[1] // narrow_count))
        elif kind == "narrow":
            block_list.append(blocks_rows_narrow(item, wide_count, narrow_count))
            local_shapes.append((item.shape[0] // narrow_count, item.shape[1] // wide_count))
        else:
            block_list.append(blocks_gain(item, wide_count, narrow_count))
            local_shapes.append((item.shape[0] // wide_count,))
    stacked = jnp.concatenate(block_list, axis=2)
    joined = stacked.reshape(wide_count * narrow_count, stacked.shape[2])
    summed = lax.psum_scatter(joined, ("wide", "narrow"), scatter_dimension=0, tiled=True).reshape(
        -1
    )
    results = []
    offset = 0
    for shape in local_shapes:
        count = 1
        for extent in shape:
            count = count * extent
        results.append(summed[offset : offset + count].reshape(shape))
        offset = offset + count
    return (
        hidden_out,
        hidden_grad,
        results[0],
        results[1],
        results[2],
        results[3],
        results[4],
        results[5],
        results[6],
        results[7],
    )


def solution(mesh):
    in_specs = (
        P("wide", "narrow", None),
        P("wide", "narrow"),
        P("wide"),
        P(),
        P(),
        P(),
        P(),
        P(),
        P(),
        P(),
        P(),
        P("wide", "narrow", None),
    )
    out_specs = (
        P("wide", "narrow", None),
        P("wide", "narrow", None),
        P("wide", "narrow"),
        P("narrow", "wide"),
        P("wide"),
        P("wide", "narrow"),
        P("wide", "narrow"),
        P("wide"),
        P("wide", "narrow"),
        P("wide", "narrow"),
    )
    return jax.shard_map(
        on_device, mesh=mesh, in_specs=in_specs, out_specs=out_specs, check_vma=False
    )
```

profile of v0, /device:TPU:0, one launch (start us, length us, event | category | flops | bytes accessed | tf_op | source)
XLA Modules:
  0.0 1036.3 jit_solution(18273378319542742261)
XLA Ops:
  10.6 5.9 copy.111
  24.7 6.3 all-to-all-start
  36.9 14.2 %all-to-all-done = bf16[2,256,768]{1,0,2:T(2,128)(2,1)S(1)} async-done(((bf16[2,256,768]{1,0,2:T(2,128)(2,1)}), bf16[2,256,768]{1,0,2:T(2,128)(2,1)S(1)}, u32[]{:S(2)}, u32[]{:S(2)}) %all-to-all-start) | async-done | bytes 786464 | tf_op jit(solution)/shard_map/all_to_all | solution.py:178
  51.1 3.5 all-to-all-start.1
  57.5 16.7 %all-to-all-done.1 = bf16[2,256,768]{1,0,2:T(2,128)(2,1)S(1)} async-done(((bf16[2,256,768]{1,0,2:T(2,128)(2,1)}), bf16[2,256,768]{1,0,2:T(2,128)(2,1)S(1)}, u32[]{:S(2)}, u32[]{:S(2)}) %all-to-all-start.1) | async-done | bytes 786464 | tf_op jit(solution)/shard_map/all_to_all | solution.py:176
  74.2 4.4 all-to-all-start.2
  85.3 13.0 %all-to-all-done.2 = bf16[2,256,768]{1,0,2:T(2,128)(2,1)} async-done(((bf16[2,256,768]{1,0,2:T(2,128)(2,1)}), bf16[2,256,768]{1,0,2:T(2,128)(2,1)}, u32[]{:S(2)}, u32[]{:S(2)}) %all-to-all-start.2) | async-done | bytes 786464 | tf_op jit(solution)/shard_map/all_to_all | solution.py:177
  98.3 2.6 copy.118
  100.9 2.5 all_to_all.95
  104.4 17.3 %while.26 = (s32[]{:T(128)}, bf16[2,1024,192]{1,2,0:T(8,128)(2,1)}, f32[2,3,1024,1]{2,1,3,0:T(4,128)}, bf16[2,1024,192]{1,2,0:T(8,128)(2,1)S(1)}, bf16[2,1024,19...) while((s32[]{:T(128)}, bf16[2,1024,192]{1,2,0:T(8,128)(2,1)}, ...), condition=%wide.region_5.6_spmd, body=%wide.region_2.5_spmd.sunk | while | flops 833811456 | bytes 48861340 | solution.py:180
  109.4 2.7 fusion.147
  118.1 2.7 fusion.147
  121.7 3.6 copy.119
  125.3 4.6 all-to-all-start.3
  130.0 7.9 fusion.85
  137.8 17.4 %all-to-all-done.3 = bf16[2,1024,192]{2,0,1:T(2,128)(2,1)} async-done(((bf16[2,1024,192]{2,0,1:T(2,128)(2,1)}), bf16[2,1024,192]{2,0,1:T(2,128)(2,1)}, u32[]{:S(2)}, u32[]{:S(2)}) %all-to-all-start.3) | async-done | bytes 786464 | tf_op jit(solution)/shard_map/all_to_all | solution.py:181
  155.2 3.8 copy.160
  160.3 2.9 fusion.82
  163.9 12.8 %fusion.27 = (bf16[3072,512]{0,1:T(8,128)(2,1)}, bf16[3072,512]{0,1:T(8,128)(2,1)}, f32[512,3072]{1,0:T(8,128)}) fusion(f32[512,3072]{1,0:T(8,128)S(1)} %copy-done.64, bf16[512,768]{1,0:T(8,128)(2,1)S(1)} %bitcast.357, bf16[768,3072]{1,0:T(8,128)(2,1)} %param.25), kind=kOutput, calls=%fused_computation.51 | convolution fusion | flops 2450522112 | bytes 24379392 | tf_op jit(solution)/shard_map/dot_general | solution.py:193
  176.7 8.4 fusion.34
  185.2 6.0 fusion.33
  199.8 2.3 copy.123
  202.1 22.1 %all_to_all.114 = bf16[2,256,768]{1,0,2:T(2,128)(2,1)S(1)} all-to-all(bf16[2,256,768]{1,0,2:T(2,128)(2,1)S(1)} %copy.123), channel_id=1, replica_groups=mesh['wide'=8,'narrow'=4] {'narrow'}, dimensions={2} | all-to-all | bytes 1572864 | tf_op jit(solution)/shard_map/all_to_all | solution.py:217
  228.2 46.5 %while.27 = (s32[]{:T(128)}, bf16[2,1024,192]{1,2,0:T(8,128)(2,1)}, bf16[2,1024,192]{1,2,0:T(8,128)(2,1)}, bf16[2,1024,192]{1,2,0:T(8,128)(2,1)}, bf16[2,1024,19...) while((s32[]{:T(128)}, bf16[2,1024,192]{1,2,0:T(8,128)(2,1)}, ...), condition=%wide.region_12.13_spmd, body=%wide.region_10.12_spmd.sunk | while | flops 2051994624 | bytes 144789888 | solution.py:218
  232.0 3.8 multiply_reduce_fusion.9
  235.7 5.3 multiply_convert_fusion.8
  241.0 4.1 fusion.159
  255.2 3.8 multiply_reduce_fusion.9
  259.0 5.3 multiply_convert_fusion.8
  264.3 4.1 fusion.159
  274.7 3.7 copy.130
  278.4 3.5 all-to-all-start.7
  284.0 22.7 %all-to-all-done.7 = bf16[2,1024,192]{2,0,1:T(2,128)(2,1)S(1)} async-done(((bf16[2,1024,192]{2,0,1:T(2,128)(2,1)}), bf16[2,1024,192]{2,0,1:T(2,128)(2,1)S(1)}, u32[]{:S(2)}, u32[]{:S(2)}) %all-to-all-start.7) | async-done | bytes 786464 | tf_op jit(solution)/shard_map/all_to_all | solution.py:224
  306.7 3.7 all-to-all-start.5
  312.7 2.3 copy.143
  316.0 2.3 copy.140
  318.3 3.6 copy.128
  321.9 13.7 %all-to-all-done.5 = bf16[2,1024,192]{2,0,1:T(2,128)(2,1)S(1)} async-done(((bf16[2,1024,192]{2,0,1:T(2,128)(2,1)}), bf16[2,1024,192]{2,0,1:T(2,128)(2,1)S(1)}, u32[]{:S(2)}, u32[]{:S(2)}) %all-to-all-start.5) | async-done | bytes 786464 | tf_op jit(solution)/shard_map/all_to_all | solution.py:222
  335.6 4.2 all-to-all-start.6
  339.9 3.8 convolution_bitcast_fusion.2
  343.7 3.8 concatenate.38
  347.8 4.7 copy.161
  352.4 4.5 fusion.87
  357.0 9.0 copy.168
  366.0 4.8 copy.162
  370.8 6.9 convolution_bitcast_fusion
  377.7 11.5 %copy.145 = f32[8,4,384,192]{3,2,1,0:T(8,128)} copy(f32[8,4,384,192]{2,3,1,0:T(8,128)} %convolution_bitcast_fusion) | data formatting | bytes 18874368 | tf_op jit(solution)/shard_map/transpose | solution.py:108
  389.2 11.2 %concatenate.41 = f32[32,73728]{1,0:T(8,128)} reshape(f32[8,4,384,192]{3,2,1,0:T(8,128)} %copy.145) | data formatting | bytes 18874368 | tf_op jit(solution)/shard_map/concatenate | solution.py:306
  401.9 3.8 copy.129
  410.3 2.3 fusion.49
  417.2 2.6 fusion.80
  419.8 2.5 copy.138
  424.8 2.5 concatenate.34
  428.2 3.6 reshape.321
  431.8 3.8 copy.136
  435.5 3.6 concatenate.35
  440.2 4.3 convolution_bitcast_fusion.1
  444.5 8.6 concatenate.37
  456.0 20.7 %dynamic-update-slice.3 = f32[32,243904]{1,0:T(8,128)} dynamic-update-slice(f32[32,243904]{1,0:T(8,128)} %dynamic-update-slice.2, f32[32,55296]{1,0:T(8,128)} %concatenate.37, s32[]{} %constant.108, s32[]{} %constant.111) | dynamic-update-slice | bytes 14155780
  476.7 8.9 dynamic-update-slice.4
  487.1 28.8 %dynamic-update-slice.6 = f32[32,243904]{1,0:T(8,128)} dynamic-update-slice(f32[32,243904]{1,0:T(8,128)} %dynamic-update-slice.5, f32[32,73728]{1,0:T(8,128)} %bitcast.326, s32[]{} %constant.108, s32[]{} %constant.114) | dynamic-update-slice | bytes 18874372
  515.9 28.5 %dynamic-update-slice.7 = f32[32,243904]{1,0:T(8,128)} dynamic-update-slice(f32[32,243904]{1,0:T(8,128)} %dynamic-update-slice.6, f32[32,73728]{1,0:T(8,128)} %concatenate.41, s32[]{} %constant.108, s32[]{} %constant.115) | dynamic-update-slice | bytes 18874372 | tf_op jit(solution)/shard_map/concatenate | solution.py:306
  544.4 469.8 %all-reduce.7.cloned.1.call-done = f32[32,243904]{1,0:T(8,128)} async-done(((f32[32,243904]{1,0:T(8,128)}), f32[32,243904]{1,0:T(8,128)}) %all-reduce.7.cloned.1.call-update) | async-done | bytes 31219728
  1022.1 4.1 dynamic-slice_reduce_fusion
  (295 shorter events, 110.1 us)
Async XLA Ops:
  7.2 153.1 %copy-start = (bf16[768,768]{1,0:T(8,128)(2,1)S(1)}, bf16[768,768]{1,0:T(8,128)(2,1)}, u32[]{:S(2)}) copy-start(bf16[768,768]{1,0:T(8,128)(2,1)} %param.23) | copy-start | bytes 3538948
  10.6 6.6 copy-start.40
  10.6 6.6 copy-start.44
  10.6 5.9 copy-start.60
  10.6 5.9 copy-start.2
  10.6 6.6 copy-start.9
  16.6 4.1 copy-start.42
  16.8 4.0 copy-start.46
  17.1 3.6 copy-start.53
  17.2 3.6 copy-start.48
  22.9 8.1 copy-start.62
  24.7 26.4 %all-to-all-start = ((bf16[2,256,768]{1,0,2:T(2,128)(2,1)}), bf16[2,256,768]{1,0,2:T(2,128)(2,1)S(1)}, u32[]{:S(2)}, u32[]{:S(2)}) async-start(bf16[2,256,768]{1,0,2:T(2,128)(2,1)} %copy.112), calls=%async_computation | async-start | bytes 1572864 | tf_op jit(solution)/shard_map/all_to_all | solution.py:178
  31.4 2.3 copy-start.36
  31.4 2.3 copy-start.38
  51.1 23.1 %all-to-all-start.1 = ((bf16[2,256,768]{1,0,2:T(2,128)(2,1)}), bf16[2,256,768]{1,0,2:T(2,128)(2,1)S(1)}, u32[]{:S(2)}, u32[]{:S(2)}) async-start(bf16[2,256,768]{1,0,2:T(2,128)(2,1)} %copy.115), calls=%async_computation.1 | async-start | bytes 1572864 | tf_op jit(solution)/shard_map/all_to_all | solution.py:176
  74.2 24.1 %all-to-all-start.2 = ((bf16[2,256,768]{1,0,2:T(2,128)(2,1)}), bf16[2,256,768]{1,0,2:T(2,128)(2,1)}, u32[]{:S(2)}, u32[]{:S(2)}) async-start(bf16[2,256,768]{1,0,2:T(2,128)(2,1)} %copy.117), calls=%async_computation.2 | async-start | bytes 1572864 | tf_op jit(solution)/shard_map/all_to_all | solution.py:177
  109.4 2.7 copy-start.28
  118.0 2.7 copy-start.28
  121.7 8.3 copy-start.61
  125.3 29.9 %all-to-all-start.3 = ((bf16[2,1024,192]{2,0,1:T(2,128)(2,1)}), bf16[2,1024,192]{2,0,1:T(2,128)(2,1)}, u32[]{:S(2)}, u32[]{:S(2)}) async-start(bf16[2,1024,192]{2,0,1:T(2,128)(2,1)} %copy.119), calls=%async_computation.3 | async-start | bytes 2097152 | tf_op jit(solution)/shard_map/all_to_all | solution.py:181
  160.3 3.6 copy-start.64
  160.3 3.2 copy-start.50
  160.3 16.4 %slice-start.2 = ((s8[4718592]{0:T(1024)(128)(4,1)}), s8[4194304]{0:T(1024)(128)(4,1)S(1)}, s32[]{:S(2)}) async-start(s8[4718592]{0:T(1024)(128)(4,1)} %bitcast.371), calls=%async_computation.11 | async-start | bytes 8388608
  163.5 21.6 %slice-start.4 = ((s8[4718592]{0:T(1024)(128)(4,1)}), s8[4194304]{0:T(1024)(128)(4,1)S(1)}, s32[]{:S(2)}) async-start(s8[4718592]{0:T(1024)(128)(4,1)} %bitcast.373), calls=%async_computation.13 | async-start | bytes 8388608
  163.9 12.8 %copy-start.31 = (bf16[2,256,768]{2,1,0:T(8,128)(2,1)}, bf16[2,256,768]{2,1,0:T(8,128)(2,1)S(1)}, u32[]{:S(2)}) copy-start(bf16[2,256,768]{2,1,0:T(8,128)(2,1)S(1)} %add_convert_fusion.2) | copy-start | bytes 2359300
  163.9 12.8 %slice-start.3 = ((s8[4718592]{0:T(1024)(128)(4,1)}), s8[524288]{0:T(1024)(128)(4,1)S(1)}, s32[]{:S(2)}) async-start(s8[4718592]{0:T(1024)(128)(4,1)} %bitcast.371), calls=%async_computation.12 | async-start | bytes 1048576
  163.9 21.2 %slice-start.5 = ((s8[4718592]{0:T(1024)(128)(4,1)}), s8[524288]{0:T(1024)(128)(4,1)S(1)}, s32[]{:S(2)}) async-start(s8[4718592]{0:T(1024)(128)(4,1)} %bitcast.373), calls=%async_computation.14 | async-start | bytes 1048576
  191.2 3.5 copy-start.12
  192.7 3.6 copy-start.10
  196.3 3.5 copy-start.55
  229.3 2.6 copy-start.5
  241.0 4.1 copy-start.21
  245.1 2.5 slice-start
  245.1 2.3 copy-start.22
  245.1 3.1 slice-start.1
  252.6 2.6 copy-start.5
  264.3 4.1 copy-start.21
  268.3 2.5 slice-start
  268.4 2.3 copy-start.22
  268.4 3.1 slice-start.1
  274.7 7.2 copy-start.23
  278.4 28.3 %all-to-all-start.7 = ((bf16[2,1024,192]{2,0,1:T(2,128)(2,1)}), bf16[2,1024,192]{2,0,1:T(2,128)(2,1)S(1)}, u32[]{:S(2)}, u32[]{:S(2)}) async-start(bf16[2,1024,192]{2,0,1:T(2,128)(2,1)} %copy.130), calls=%async_computation.7 | async-start | bytes 2097152 | tf_op jit(solution)/shard_map/all_to_all | solution.py:224
  282.0 33.1 %copy-start.8 = (bf16[2,4,256,192]{2,1,3,0:T(4,128)(2,1)S(1)}, bf16[2,4,256,192]{2,1,3,0:T(4,128)(2,1)}, u32[]{:S(2)}) copy-start(bf16[2,4,256,192]{2,1,3,0:T(4,128)(2,1)} %copy.160) | copy-start | bytes 2359300
  306.7 28.9 %all-to-all-start.5 = ((bf16[2,1024,192]{2,0,1:T(2,128)(2,1)}), bf16[2,1024,192]{2,0,1:T(2,128)(2,1)S(1)}, u32[]{:S(2)}, u32[]{:S(2)}) async-start(bf16[2,1024,192]{2,0,1:T(2,128)(2,1)} %copy.126), calls=%async_computation.5 | async-start | bytes 2097152 | tf_op jit(solution)/shard_map/all_to_all | solution.py:222
  335.6 8.1 copy-start.16
  335.6 66.3 %all-to-all-start.6 = ((bf16[2,1024,192]{2,0,1:T(2,128)(2,1)}), bf16[2,1024,192]{2,0,1:T(2,128)(2,1)}, u32[]{:S(2)}, u32[]{:S(2)}) async-start(bf16[2,1024,192]{2,0,1:T(2,128)(2,1)} %copy.128), calls=%async_computation.6 | async-start | bytes 2097152 | tf_op jit(solution)/shard_map/all_to_all | solution.py:223
  339.8 674.4 %all-reduce.7.cloned.1.call-start = ((), (), s32[]{:S(2)}) async-start(), calls=%async_computation.8 | async-start | bytes 62455808
  343.7 3.8 copy-start.57
  343.7 3.8 copy-start.32
  366.0 4.8 copy-start.35
  389.2 11.9 %copy-start.17 = (bf16[2,1024,192]{2,0,1:T(2,128)(2,1)S(1)}, bf16[2,1024,192]{2,0,1:T(2,128)(2,1)}, u32[]{:S(2)}) copy-start(bf16[2,1024,192]{2,0,1:T(2,128)(2,1)} %copy-done.16) | copy-start | bytes 2359300
  400.3 5.4 copy-start.37
  400.3 5.4 copy-start.39
  410.3 2.4 copy-start.54
  410.3 2.4 copy-start.49
  410.3 3.5 copy-start.11
  410.3 3.5 copy-start.13
  410.3 3.5 copy-start.14
  410.3 3.5 copy-start.56
  414.0 3.1 copy-start.59
  417.2 5.1 copy-start.63
  444.5 8.6 copy-start.6
  456.0 20.7 %copy-start.7 = (f32[32,18432]{1,0:T(8,128)S(1)}, f32[32,18432]{1,0:T(8,128)}, u32[]{:S(2)}) copy-start(f32[32,18432]{1,0:T(8,128)} %concatenate.38) | copy-start | bytes 7077892
  544.4 484.8 %copy-start.1 = (bf16[768,768]{1,0:T(8,128)(2,1)S(1)}, bf16[768,768]{1,0:T(8,128)(2,1)}, u32[]{:S(2)}) copy-start(bf16[768,768]{1,0:T(8,128)(2,1)} %param.23) | copy-start | bytes 3538948
  (26 other events, 43.9 us)
Sparse Core Ops, SparseCore 0:
  544.5 469.6 all-reduce.6
where the time goes:
time: 1050 us; the launch traced here: 1040 us
  waiting for transfers between devices  568 us (54%)
  local copies, waits for them, and re-layouts  259 us (25%)
  matrix products  107 us (10%)
  other arithmetic  34.5 us (3%)
  starting transfers between devices  30.4 us (3%)
  blocking collectives  22.1 us (2%)
  between operations  15.2 us (1%)
    unnamed x2, waiting for transfers between devices  470 us
    unnamed x139, local copies, waits for them, and re-layouts  85.9 us
    concatenate x6, local copies, waits for them, and re-layouts, on_device(): stacked = jnp.concatenate(block_list, axis=2)  58.1 us
    all_to_all x1, waiting for transfers between devices, on_device(): lax.all_to_all(d_value_heads, 'narrow', split_axis=1, concat_axis=2, tile...  22.7 us
    all_to_all x1, blocking collectives, on_device(): lax.all_to_all(d_attended, 'narrow', split_axis=2, concat_axis=1, tiled=T...  22.1 us
  transfers between devices with their start and end apart: 8, of which 7 were waited for; matrix products, arithmetic and copies ran while one was open for 9% of the time, Pallas kernels for 0%

commit v1 on v0

v1 whole, which is shorter than its diff:
```python
import jax
import jax.numpy as jnp
from jax import lax
from jax.sharding import PartitionSpec as P

HEAD_DIM = 64
HIGHEST = lax.Precision.HIGHEST
norm_eps = 1e-05
AXES = ("wide", "narrow")
F32 = jnp.float32
BF16 = jnp.bfloat16


def dot(left, right):
    return jnp.dot(left, right, preferred_element_type=F32)


def tdot(left, right):
    return lax.dot_general(left, right, (((0,), (0,)), ((), ())), preferred_element_type=F32)


def ndot(left, right):
    return lax.dot_general(left, right, (((1,), (1,)), ((), ())), preferred_element_type=F32)


def gelu_tanh(values):
    return jax.nn.gelu(values, approximate=True)


def pairs(wide, narrow, target):
    result = []
    for w in range(wide):
        for n in range(narrow):
            w_to, n_to = target(w, n)
            result.append((w * narrow + n, w_to * narrow + n_to))
    return result


def inverse(table):
    return [(target, source) for source, target in table]


def rotate(values, cosine, sine, sign):
    half = HEAD_DIM // 2
    first = values[..., :half]
    second = values[..., half:]
    return jnp.concatenate(
        [first * cosine - sign * second * sine, second * cosine + sign * first * sine], axis=-1
    )


def normalize(hidden):
    center = hidden - jnp.mean(hidden, axis=-1, keepdims=True)
    variance = jnp.mean(center * center, axis=-1, keepdims=True)
    inverse_std = lax.rsqrt(variance + norm_eps)
    return center * inverse_std, inverse_std


def normalize_back(grad, xhat, inverse_std):
    mean_grad = jnp.mean(grad, axis=-1, keepdims=True)
    mean_both = jnp.mean(grad * xhat, axis=-1, keepdims=True)
    return (grad - mean_grad - xhat * mean_both) * inverse_std


def make(wide, narrow):
    wide_bits = wide.bit_length() - 1

    def first_message(w, n):
        p, c = w // 2, w % 2
        return 2 * p + n // 2, 2 * c + n % 2

    def second_message(w, n):
        p, c = w // 2, w % 2
        return 2 * p + n // 2, 2 * c + 1 - n % 2

    message_one = pairs(wide, narrow, first_message)
    message_two = pairs(wide, narrow, second_message)
    flip = [pairs(wide, narrow, lambda w, n, b=b: (w ^ (1 << b), n)) for b in range(wide_bits)]
    narrow_near = pairs(wide, narrow, lambda w, n: (w, n ^ 1))
    narrow_far = pairs(wide, narrow, lambda w, n: (w, narrow - 1 - n))

    def on_device(
        hidden_in,
        positions,
        time_index,
        cond_table,
        ada_weight,
        norm1_gain,
        qkv_weight,
        out_weight,
        norm2_gain,
        up_weight,
        down_weight,
        cotangent,
    ):
        w = lax.axis_index("wide")
        n = lax.axis_index("narrow")
        core = w % 2
        part_len, width = hidden_in.shape[1:]
        heads = width // HEAD_DIM
        odd = n % 2

        def take(array, index):
            return lax.dynamic_index_in_dim(array, index, axis=0, keepdims=False)

        def spread(array):
            one = lax.ppermute(take(array, odd), AXES, message_one)
            two = lax.ppermute(take(array, 1 - odd), AXES, message_two)
            return jnp.concatenate([one, two], axis=0)

        def gather(array):
            one = lax.ppermute(array[:part_len], AXES, inverse(message_one))
            two = lax.ppermute(array[part_len:], AXES, inverse(message_two))
            return jnp.stack([jnp.where(odd == 0, one, two), jnp.where(odd == 0, two, one)])

        def reduce_blocks(array, order):
            block = array.shape[2:]
            current = array.reshape((2,) * wide_bits + (narrow,) + block)
            axes = list(range(wide_bits - 1, -1, -1))
            for bit in order:
                axis = axes.index(bit)
                mine = (w >> bit) & 1
                send = lax.dynamic_index_in_dim(current, 1 - mine, axis=axis, keepdims=False)
                keep = lax.dynamic_index_in_dim(current, mine, axis=axis, keepdims=False)
                received = lax.ppermute(send, AXES, flip[bit])
                current = (keep.astype(F32) + received.astype(F32)).astype(BF16)
                axes.pop(axis)
            near = n ^ 1
            send = jnp.stack([take(current, near), take(current, narrow - 1 - near)])
            keep = jnp.stack([take(current, n), take(current, narrow - 1 - n)])
            received = lax.ppermute(send, AXES, narrow_near)
            current = keep.astype(F32) + received.astype(F32)
            received = lax.ppermute(current[1].astype(BF16), AXES, narrow_far)
            return current[0] + received.astype(F32)

        hidden = spread(hidden_in).astype(F32)
        place = spread(positions)
        d_out = spread(cotangent).astype(F32)
        other_time = lax.ppermute(time_index, AXES, flip[0])
        row_time = jnp.where(n // 2 == core, time_index[n % 2], other_time[n % 2])
        embedded = lax.dynamic_slice_in_dim(cond_table, row_time, 1, axis=0).astype(F32)
        gate = jax.nn.sigmoid(embedded)
        condition = (embedded * gate).astype(BF16)
        modulation = dot(condition, ada_weight).reshape(6, 1, width)
        shift_one, scale_one, gate_one, shift_two, scale_two, gate_two = modulation
        gain_one = norm1_gain.astype(F32)
        gain_two = norm2_gain.astype(F32)
        tokens = hidden.shape[0]

        xhat_one, std_one = normalize(hidden)
        norm_one = (xhat_one * gain_one * (1.0 + scale_one) + shift_one).astype(BF16)
        qkv = dot(norm_one, qkv_weight)
        half = HEAD_DIM // 2
        frequency = 10000.0 ** (-jnp.arange(half, dtype=F32) / half)
        angles = place.astype(F32)[:, None, None] * frequency
        cosine, sine = jnp.cos(angles), jnp.sin(angles)

        def rotated(part, sign):
            return (
                rotate(part.reshape(tokens, heads, HEAD_DIM), cosine, sine, sign)
                .reshape(tokens, width)
                .astype(BF16)
            )

        queries = rotated(qkv[:, :width], 1.0)
        keys = rotated(qkv[:, width : 2 * width], 1.0)
        values = qkv[:, 2 * width :].astype(BF16)
        mine = jnp.concatenate([keys, values], axis=1)
        other = lax.ppermute(mine, AXES, flip[0])
        both = jnp.concatenate([mine, other], axis=0)

        group = 3

        def split_heads(array):
            return array.reshape(-1, heads // group, group, HEAD_DIM).transpose(1, 2, 0, 3)

        def join_heads(array):
            return array.transpose(2, 0, 1, 3).reshape(-1, width)

        q_heads = split_heads(queries)
        k_heads = split_heads(both[:, :width])
        v_heads = split_heads(both[:, width:])

        def attend(item):
            q, k, v = item
            scores = jnp.einsum("hqd,hkd->hqk", q, k, preferred_element_type=F32) * HEAD_DIM**-0.5
            row_max = jnp.max(scores, axis=-1, keepdims=True)
            expo = jnp.exp(scores - row_max)
            total = jnp.sum(expo, axis=-1, keepdims=True)
            probs = (expo / total).astype(BF16)
            result = jnp.einsum("hqk,hkd->hqd", probs, v, preferred_element_type=F32)
            return result.astype(BF16), row_max + jnp.log(total)

        attended_heads, log_total = lax.map(attend, (q_heads, k_heads, v_heads))
        attended = join_heads(attended_heads)
        projected = dot(attended, out_weight)
        middle = hidden + gate_one * projected
        xhat_two, std_two = normalize(middle)
        norm_two = (xhat_two * gain_two * (1.0 + scale_two) + shift_two).astype(BF16)
        up = dot(norm_two, up_weight)
        activated, gelu_back = jax.vjp(gelu_tanh, up)
        activated = activated.astype(BF16)
        down = dot(activated, down_weight)
        hidden_out = gather((middle + gate_two * down).astype(BF16))
        d_gate_two = jnp.sum(d_out * down, axis=0)
        d_down = (d_out * gate_two).astype(BF16)
        grad_down = tdot(activated, d_down)
        d_up = gelu_back(ndot(d_down, down_weight))[0].astype(BF16)
        grad_up = tdot(norm_two, d_up)
        d_norm_two = ndot(d_up, up_weight)
        d_shift_two = jnp.sum(d_norm_two, axis=0)
        sum_two = jnp.sum(d_norm_two * xhat_two, axis=0)
        grad_gain_two = sum_two * (1.0 + scale_two[0])
        d_scale_two = sum_two * gain_two
        d_middle = d_out + normalize_back(
            d_norm_two * (gain_two * (1.0 + scale_two)), xhat_two, std_two
        )
        d_gate_one = jnp.sum(d_middle * projected, axis=0)
        d_projected = (d_middle * gate_one).astype(BF16)
        grad_out = tdot(attended, d_projected)
        d_attended = ndot(d_projected, out_weight).astype(BF16)

        def attend_back(item):
            q, k, v, d_result, total = item
            scores = jnp.einsum("hqd,hkd->hqk", q, k, preferred_element_type=F32) * HEAD_DIM**-0.5
            probs = jnp.exp(scores - total)
            d_v = jnp.einsum("hqk,hqd->hkd", probs.astype(BF16), d_result, preferred_element_type=F32)
            d_probs = jnp.einsum("hqd,hkd->hqk", d_result, v, preferred_element_type=F32)
            d_scores = probs * (d_probs - jnp.sum(probs * d_probs, axis=-1, keepdims=True))
            d_low = d_scores.astype(BF16)
            d_q = jnp.einsum("hqk,hkd->hqd", d_low, k, preferred_element_type=F32) * HEAD_DIM**-0.5
            d_k = jnp.einsum("hqk,hqd->hkd", d_low, q, preferred_element_type=F32) * HEAD_DIM**-0.5
            return d_q.astype(BF16), d_k.astype(BF16), d_v.astype(BF16)

        d_q_heads, d_k_heads, d_v_heads = lax.map(
            attend_back, (q_heads, k_heads, v_heads, split_heads(d_attended), log_total)
        )
        d_query = join_heads(d_q_heads)
        d_both = jnp.concatenate([join_heads(d_k_heads), join_heads(d_v_heads)], axis=1)
        received = lax.ppermute(d_both[tokens:], AXES, flip[0])
        d_mine = (d_both[:tokens].astype(F32) + received.astype(F32)).astype(BF16)
        d_qkv = jnp.concatenate(
            [
                rotated(d_query.astype(F32), -1.0),
                rotated(d_mine[:, :width].astype(F32), -1.0),
                d_mine[:, width:],
            ],
            axis=1,
        )
        grad_qkv = tdot(norm_one, d_qkv)
        d_norm_one = ndot(d_qkv, qkv_weight)
        d_shift_one = jnp.sum(d_norm_one, axis=0)
        sum_one = jnp.sum(d_norm_one * xhat_one, axis=0)
        grad_gain_one = sum_one * (1.0 + scale_one[0])
        d_scale_one = sum_one * gain_one
        hidden_grad = d_middle + normalize_back(
            d_norm_one * (gain_one * (1.0 + scale_one)), xhat_one, std_one
        )
        hidden_grad = gather(hidden_grad.astype(BF16))

        d_modulation = jnp.concatenate(
            [d_shift_one, d_scale_one, d_gate_one, d_shift_two, d_scale_two, d_gate_two]
        )[None, :]
        d_condition = lax.dot_general(
            d_modulation,
            ada_weight.astype(F32),
            (((1,), (1,)), ((), ())),
            precision=HIGHEST,
            preferred_element_type=F32,
        )
        d_embedded = d_condition * gate * (1.0 + embedded * (1.0 - gate))
        times = cond_table.shape[0]
        grad_table = jnp.where(
            jnp.arange(times, dtype=jnp.int32)[:, None] == row_time, d_embedded, 0.0
        )
        grad_ada = condition.astype(F32).T * d_modulation

        def blocks(grad):
            rows, cols = grad.shape
            split = grad.astype(BF16).reshape(wide, rows // wide, narrow, cols // narrow)
            return split.transpose(0, 2, 1, 3).reshape(wide, narrow, -1, 128)

        def blocks_other(grad):
            rows, cols = grad.shape
            split = grad.astype(BF16).reshape(narrow, rows // narrow, wide, cols // wide)
            return split.transpose(2, 0, 1, 3).reshape(wide, narrow, -1)

        def blocks_gain(grad):
            split = grad.astype(BF16).reshape(wide, 1, -1)
            return jnp.broadcast_to(split, (wide, narrow, split.shape[2]))

        rest = jnp.concatenate(
            [
                blocks(grad_table).reshape(wide, narrow, -1),
                blocks_other(grad_ada),
                blocks_gain(grad_gain_one),
                blocks_gain(grad_gain_two),
            ],
            axis=2,
        )
        up_order = list(range(wide_bits))
        down_order = [0] + list(range(wide_bits - 1, 0, -1))
        sum_down = reduce_blocks(blocks(grad_down), down_order)
        sum_up = reduce_blocks(blocks(grad_up), up_order)
        sum_out = reduce_blocks(blocks(grad_out), up_order)
        sum_qkv = reduce_blocks(blocks(grad_qkv), down_order)
        sum_rest = reduce_blocks(rest, up_order)

        def block_shape(array):
            return array.shape[0] // wide, array.shape[1] // narrow

        table_count = times // wide * (cond_table.shape[1] // narrow)
        ada_shape = (ada_weight.shape[0] // narrow, ada_weight.shape[1] // wide)
        ada_count = ada_shape[0] * ada_shape[1]
        gain_count = width // wide
        at = table_count + ada_count
        return (
            hidden_out,
            hidden_grad,
            sum_rest[:table_count].reshape(block_shape(cond_table)),
            sum_rest[table_count:at].reshape(ada_shape),
            sum_rest[at : at + gain_count],
            sum_qkv.reshape(block_shape(qkv_weight)),
            sum_out.reshape(block_shape(out_weight)),
            sum_rest[at + gain_count :],
            sum_up.reshape(block_shape(up_weight)),
            sum_down.reshape(block_shape(down_weight)),
        )

    return on_device


def solution(mesh):
    in_specs = (
        P("wide", "narrow", None),
        P("wide", "narrow"),
        P("wide"),
        P(),
        P(),
        P(),
        P(),
        P(),
        P(),
        P(),
        P(),
        P("wide", "narrow", None),
    )
    out_specs = (
        P("wide", "narrow", None),
        P("wide", "narrow", None),
        P("wide", "narrow"),
        P("narrow", "wide"),
        P("wide"),
        P("wide", "narrow"),
        P("wide", "narrow"),
        P("wide"),
        P("wide", "narrow"),
        P("wide", "narrow"),
    )
    return jax.shard_map(
        make(mesh.shape["wide"], mesh.shape["narrow"]),
        mesh=mesh,
        in_specs=in_specs,
        out_specs=out_specs,
        check_vma=False,
    )
```

time: 1050 us -> 565 us (0.54)
  waiting for transfers between devices: 568 us -> 90 us
  local copies, waits for them, and re-layouts: 259 us -> 190 us
  other arithmetic: 34.5 us -> 73.1 us
  starting transfers between devices: 30.4 us -> 66.1 us
  matrix products: 107 us -> 132 us
  blocking collectives: 22.1 us -> 0 us
  between operations: 15.2 us -> 3.4 us
    unnamed x2 -> x0, waiting for transfers between devices: 470 us -> none
    all_to_all x7 -> x0, waiting for transfers between devices: 97.7 us -> none  [the longest x1 22.7 us: on_device(): lax.all_to_all(d_value_heads, 'narrow', split_axis=1, concat_axis=2, tile...]
    ppermute x0 -> x38, waiting for transfers between devices: none -> 90 us  [the longest x15 69.1 us: reduce_blocks(): received = lax.ppermute(send, AXES, flip[bit])]
    unnamed x139 -> x122, local copies, waits for them, and re-layouts: 85.9 us -> 17.6 us
    ppermute x0 -> x38, starting transfers between devices: none -> 66.1 us  [the longest x5 17.1 us: reduce_blocks(): received = lax.ppermute(current[1].astype(BF16), AXES, narrow_far)]
    concatenate x7 -> x3, local copies, waits for them, and re-layouts: 58.1 us -> 8.57 us  [the longest x1 5.95 us: on_device(): jnp.concatenate([blocks(grad_table).reshape(wide, narrow, -1), blocks_oth...]
    reshape x8 -> x11, local copies, waits for them, and re-layouts: 9.09 us -> 44.9 us  [the longest x6 36.4 us: blocks(): grad.astype(BF16).reshape(wide, rows // wide, narrow, cols // narrow)]
    another operation x4 -> x6, local copies, waits for them, and re-layouts: 3.95 us -> 35.4 us  [the longest x4 33.5 us: reduce_blocks(): current = array.reshape((2,) * wide_bits + (narrow,) + block)]
  transfers between devices with their start and end apart: 8 -> 38, of which waited for: 7 -> 15; matrix products, arithmetic and copies ran while one was open for 9% -> 52% of each run, Pallas kernels for 0% -> 0%
where the time goes in v1:
time: 565 us; the launch traced here: 555 us
  local copies, waits for them, and re-layouts  190 us (34%)
  matrix products  132 us (23%)
  waiting for transfers between devices  90 us (16%)
  other arithmetic  73.1 us (13%)
  starting transfers between devices  66.1 us (12%)
    ppermute x15, waiting for transfers between devices, reduce_blocks(): received = lax.ppermute(send, AXES, flip[bit])  69.1 us
    reshape x6, local copies, waits for them, and re-layouts, blocks(): grad.astype(BF16).reshape(wide, rows // wide, narrow, cols // narrow)  36.4 us
    another operation x4, local copies, waits for them, and re-layouts, reduce_blocks(): current = array.reshape((2,) * wide_bits + (narrow,) + block)  33.5 us
    dot_general x4, matrix products, tdot(): lax.dot_general(left, right, (((0,), (0,)), ((), ())), preferred_element_...  20.4 us
    dot_general x5, matrix products, dot(): return jnp.dot(left, right, preferred_element_type=F32)  19.6 us
    dot_general x4, matrix products, ndot(): lax.dot_general(left, right, (((1,), (1,)), ((), ())), preferred_element_...  18.5 us
    unnamed x122, local copies, waits for them, and re-layouts  17.6 us
    ppermute x5, starting transfers between devices, reduce_blocks(): received = lax.ppermute(current[1].astype(BF16), AXES, narrow_far)  17.1 us
  transfers between devices with their start and end apart: 38, of which 15 were waited for; matrix products, arithmetic and copies ran while one was open for 52% of the time, Pallas kernels for 0%

profile of v1, /device:TPU:0, one launch (start us, length us, event | category | flops | bytes accessed | tf_op | source)
XLA Modules:
  0.0 555.0 jit_solution(17297277156423035330)
XLA Ops:
  2.9 4.5 collective-permute-start
  7.4 3.0 collective-permute-start.1
  26.1 3.3 fusion.123
  32.2 3.1 copy.31
  35.3 3.0 copy.32
  44.3 2.7 pad_maximum_fusion.3
  47.0 6.4 %collective-permute-start.5 = (bf16[512,1536]{1,0:T(8,128)(2,1)}, bf16[512,1536]{1,0:T(8,128)(2,1)}, u32[]{:S(2)}, u32[]{:S(2)}) collective-permute-start(bf16[512,1536]{1,0:T(8,128)(2,1)} %pad_maximum_fusion.3), channel_id=1, source_target_pairs={{0,4},{1,5},{2,6},{3,7},{4,0},{5,1},{6,2},{7,3},{8,12},{9,13},{10,... | collective-permute-start | bytes 4718600 | tf_op jit(solution)/shard_map/ppermute | solution.py:169
  54.4 4.7 collective-permute-start.8
  78.2 30.2 %while.26 = (s32[]{:T(128)}, bf16[4,3,512,64]{2,3,1,0:T(8,128)(2,1)}, f32[4,3,512,1]{2,1,3,0:T(4,128)}, bf16[4,3,512,64]{2,3,1,0:T(8,128)(2,1)}, bf16[4,3,1024,6...) while((s32[]{:T(128)}, bf16[4,3,512,64]{2,3,1,0:T(8,128)(2,1)}, ...), condition=%wide.region_5.6_spmd, body=%wide.region_2.5_spmd.sunk | while | flops 416905728 | bytes 20107852 | solution.py:194
  82.3 3.4 fusion.168
  89.9 3.4 fusion.168
  97.4 3.4 fusion.168
  105.0 3.4 fusion.168
  111.8 4.9 fusion.125
  116.7 7.8 %fusion.63 = bf16[512,3072]{1,0:T(8,128)(2,1)S(1)} fusion(f32[512,3072]{1,0:T(8,128)S(1)} %fusion.125, bf16[3072,768]{1,0:T(8,128)(2,1)} %param.26, f32[768]{0:T(1024)S(1)} %get-tuple-element.214, bf16[256,768]{1,0:T(8,128)(2,1)} %collective-permute-done.9, bf16[256,768]{1,0:T(8,128)(2,1)} %collective-permute-done.8), kind=kOutput, calls=%fused_computation.68 | convolution fusion | flops 2449735680 | bytes 14945280 | tf_op jit(solution)/shard_map/dot_general | solution.py:23
  124.6 5.0 convolution_convert_fusion.1
  129.7 3.6 multiply_reduce_fusion.2
  133.2 7.1 %fusion.87 = (f32[768]{0:T(1024)}, bf16[512,768]{1,0:T(8,128)(2,1)}, f32[768]{0:T(1024)}, f32[512,768]{1,0:T(8,128)S(1)}) fusion(bf16[256,768]{1,0:T(8,128)(2,1)} %collective-permute-done.9, bf16[256,768]{1,0:T(8,128)(2,1)} %collective-permute-done.8, f32[512,768]{1,0:T(8,128)S(1)} %get-tuple-element.148, f32[768]{0:T(1024)S(1)} %get-tuple-element.214, ...), kind=kOutput, calls=%fused_computation.119 | convolution fusion | flops 2437544448 | bytes 18894848 | tf_op jit(solution)/shard_map/dot_general | solution.py:15
  140.4 3.5 convolution_convert_fusion.3
  145.6 6.6 %convolution_convert_fusion = bf16[3072,768]{1,0:T(8,128)(2,1)} fusion(f32[768]{0:T(1024)S(1)} %get-tuple-element.214, bf16[256,768]{1,0:T(8,128)(2,1)} %collective-permute-done.9, bf16[256,768]{1,0:T(8,128)(2,1)} %collective-permute-done.8, f32[512,3072]{1,0:T(8,128)S(1)} %fusion.125), kind=kOutput, calls=%fused_computation.70 | convolution fusion | flops 2434793472 | bytes 11799552 | tf_op jit(solution)/shard_map/dot_general | solution.py:19
  152.2 6.6 %copy.40 = bf16[3072,768]{0,1:T(8,128)(2,1)} copy(bf16[3072,768]{1,0:T(8,128)(2,1)} %convolution_convert_fusion) | data formatting | bytes 9437184 | tf_op jit(solution)/shard_map/convert_element_type | solution.py:280
  158.8 5.6 %copy.44 = bf16[96,8,8,384]{3,2,1,0:T(8,128)(2,1)} copy(bf16[96,8,8,384]{3,1,2,0:T(8,128)(2,1)} %bitcast.290) | data formatting | bytes 9437184
  164.4 9.1 %copy.41 = bf16[8,4,384,192]{3,2,1,0:T(8,128)(2,1)} copy(bf16[8,4,384,192]{2,0,3,1:T(8,128)(2,1)} %bitcast.292) | data formatting | bytes 9437184 | tf_op jit(solution)/shard_map/transpose | solution.py:281
  173.5 12.0 %reshape_reshape.16 = bf16[2,2,2,4,576,128]{5,4,3,2,1,0:T(8,128)(2,1)} reshape(bf16[8,4,384,192]{3,2,1,0:T(8,128)(2,1)} %copy.41) | data formatting | bytes 9437184 | tf_op jit(solution)/shard_map/reshape;reshape | solution.py:118
  185.6 3.2 dynamic-slice_bitcast_fusion.1
  189.1 9.8 %reshape.422 = bf16[8,96,4,768]{3,2,1,0:T(4,128)(2,1)} reshape(bf16[768,3072]{1,0:T(8,128)(2,1)} %convolution_convert_fusion.1) | data formatting | bytes 9437184 | tf_op jit(solution)/shard_map/reshape | solution.py:280
  198.8 5.3 copy.48
  204.2 9.4 %reshape_reshape.15 = bf16[2,2,2,4,576,128]{5,4,3,2,1,0:T(8,128)(2,1)} reshape(bf16[8,4,96,768]{3,2,1,0:T(8,128)(2,1)} %bitcast.291) | data formatting | bytes 9437184 | tf_op jit(solution)/shard_map/reshape;reshape | solution.py:118
  213.6 3.2 dynamic-slice_bitcast_fusion.2
  217.0 4.4 reshape.420
  221.4 2.9 copy.50
  224.4 4.1 reshape_reshape.14
  234.0 58.1 %while.27 = (s32[]{:T(128)}, bf16[4,3,512,64]{2,3,1,0:T(8,128)(2,1)}, bf16[4,3,1024,64]{2,3,1,0:T(8,128)(2,1)}, bf16[4,3,1024,64]{2,3,1,0:T(8,128)(2,1)}, bf16[4...) while((s32[]{:T(128)}, ...), condition=%wide.region_12.13_spmd, body=%wide.region_10.12_spmd.sunk | while | flops 1026292224 | bytes 53333124 | solution.py:235
  236.9 2.9 multiply_reduce_fusion.11
  243.7 2.8 fusion.178
  251.4 2.9 multiply_reduce_fusion.11
  258.2 2.8 fusion.178
  265.9 2.9 multiply_reduce_fusion.11
  272.8 2.8 fusion.178
  280.4 2.9 multiply_reduce_fusion.11
  287.2 2.8 fusion.178
  298.7 4.2 collective-permute-done.24
  313.7 8.0 %collective-permute-done.7 = bf16[256,768]{1,0:T(8,128)(2,1)S(1)} collective-permute-done((bf16[256,768]{1,0:T(8,128)(2,1)}, bf16[256,768]{1,0:T(8,128)(2,1)S(1)}, u32[]{:S(2)}, u32[]{:S(2)}) %collective-permute-start.7) | collective-permute-done | bytes 393248 | tf_op jit(solution)/shard_map/ppermute | solution.py:113
  323.4 8.3 %collective-permute-start.27 = (bf16[144,128]{1,0:T(8,128)(2,1)S(1)}, bf16[144,128]{1,0:T(8,128)(2,1)S(1)}, u32[]{:S(2)}, u32[]{:S(2)}) collective-permute-start(bf16[144,128]{1,0:T(8,128)(2,1)S(1)} %fusion.114), channel_id=1, source_target_pairs={{0,3},{1,2},{2,1},{3,0},{4,7},{5,6},{6,5},{7,4},{8,11},{9,10},{10,... | collective-permute-start | bytes 110600 | tf_op jit(solution)/shard_map/ppermute | solution.py:133
  341.6 5.5 fusion.84
  366.6 2.7 multiply_convert_fusion.2
  370.8 5.9 %concatenate.60 = bf16[2,2,2,4,22720]{4,3,2,1,0:T(4,128)(2,1)} concatenate(bf16[2,2,2,4,4096]{4,3,2,1,0:T(4,128)(2,1)} %select_convert_fusion, bf16[2,2,2,4,18432]{4,3,2,1,0:T(4,128)(2,1)} %multiply_convert_fusion.2, bf16[2,2,2,4,96]{4,3,2,1,0:T(4,128)(2,1)S(1)} %broadcast_in_dim.92, bf16[2,2,2,4,96]{4,3,2,1,0:T(4,128)(2,1)S(1)} %broadcast_in_dim.94), dimensions={4} | concatenate | bytes 2908160 | tf_op jit(solution)/shard_map/concatenate | solution.py:292
  384.2 4.5 collective-permute-start.11
  391.3 5.3 convolution_convert_fusion.2
  396.5 9.3 %reshape.418 = bf16[8,96,4,576]{3,2,1,0:T(4,128)(2,1)} reshape(bf16[768,2304]{1,0:T(8,128)(2,1)} %convolution_convert_fusion.2) | data formatting | bytes 7077888 | tf_op jit(solution)/shard_map/reshape | solution.py:280
  405.9 4.6 copy.49
  410.5 7.9 %reshape_reshape.13 = bf16[2,2,2,4,432,128]{5,4,3,2,1,0:T(8,128)(2,1)} reshape(bf16[8,4,96,576]{3,2,1,0:T(8,128)(2,1)} %bitcast.294) | data formatting | bytes 7077888 | tf_op jit(solution)/shard_map/reshape;reshape | solution.py:118
  418.4 2.8 dynamic-slice_bitcast_fusion.3
  426.8 3.0 fusion.64
  431.5 4.6 collective-permute-done.14
  439.2 23.8 %collective-permute-done.15 = bf16[4,22720]{1,0:T(4,128)(2,1)S(1)} collective-permute-done((bf16[4,22720]{1,0:T(4,128)(2,1)S(1)}, bf16[4,22720]{1,0:T(4,128)(2,1)S(1)}, u32[]{:S(2)}, u32[]{:S(2)}) %collective-permute-start.15) | collective-permute-done | bytes 181792 | tf_op jit(solution)/shard_map/ppermute | solution.py:125
  468.9 2.8 collective-permute-start.17
  471.9 2.9 collective-permute-done.17
  485.6 8.6 %collective-permute-done.29 = bf16[2,4,576,128]{3,2,1,0:T(8,128)(2,1)} collective-permute-done((bf16[2,4,576,128]{3,2,1,0:T(8,128)(2,1)}, bf16[2,4,576,128]{3,2,1,0:T(8,128)(2,1)}, u32[]{:S(2)}, u32[]{:S(2)}) %collective-permute-start.29) | collective-permute-done | bytes 1179680 | tf_op jit(solution)/shard_map/ppermute | solution.py:125
  498.1 6.9 %collective-permute-done.35 = bf16[4,576,128]{2,1,0:T(8,128)(2,1)S(1)} collective-permute-done((bf16[4,576,128]{2,1,0:T(8,128)(2,1)S(1)}, bf16[4,576,128]{2,1,0:T(8,128)(2,1)S(1)}, u32[]{:S(2)}, u32[]{:S(2)}) %collective-permute-start.35) | collective-permute-done | bytes 589856 | tf_op jit(solution)/shard_map/ppermute | solution.py:125
  507.0 5.2 collective-permute-done.30
  514.5 12.1 %collective-permute-done.19 = bf16[2,4,432,128]{3,2,1,0:T(8,128)(2,1)S(1)} collective-permute-done((bf16[2,4,432,128]{3,2,1,0:T(8,128)(2,1)S(1)}, bf16[2,4,432,128]{3,2,1,0:T(8,128)(2,1)S(1)}, u32[]{:S(2)}, u32[]{:S(2)}) %collective-permute-start.19) | collective-permute-done | bytes 884768 | tf_op jit(solution)/shard_map/ppermute | solution.py:125
  531.5 3.7 collective-permute-done.20
  537.7 3.7 collective-permute-done.21
  (363 shorter events, 223.8 us)
Async XLA Ops:
  0.6 25.4 %copy-start = (bf16[768,2304]{1,0:T(8,128)(2,1)S(1)}, bf16[768,2304]{1,0:T(8,128)(2,1)}, u32[]{:S(2)}) copy-start(bf16[768,2304]{1,0:T(8,128)(2,1)} %param.22) | copy-start | bytes 10616836
  0.7 9.8 %copy-start.52 = (s32[2]{0:T(128)S(1)}, s32[2]{0:T(128)}, u32[]{:S(2)}) copy-start(s32[2]{0:T(128)} %param.18) | copy-start | bytes 28
  0.7 9.8 %copy-start.51 = (s32[2,256]{1,0:T(2,128)S(1)}, s32[2,256]{1,0:T(2,128)}, u32[]{:S(2)}) copy-start(s32[2,256]{1,0:T(2,128)} %param.17) | copy-start | bytes 6148
  0.7 13.6 %copy-start.33 = (bf16[768]{0:T(1024)(128)(2,1)S(1)}, bf16[768]{0:T(1024)(128)(2,1)}, u32[]{:S(2)}) copy-start(bf16[768]{0:T(1024)(128)(2,1)} %param.21) | copy-start | bytes 4612
  0.7 18.8 %copy-start.31 = (bf16[768]{0:T(1024)(128)(2,1)S(1)}, bf16[768]{0:T(1024)(128)(2,1)}, u32[]{:S(2)}) copy-start(bf16[768]{0:T(1024)(128)(2,1)} %param.24) | copy-start | bytes 4612
  2.9 20.3 %collective-permute-start = (bf16[256,768]{1,0:T(8,128)(2,1)}, bf16[256,768]{1,0:T(8,128)(2,1)}, u32[]{:S(2)}, u32[]{:S(2)}) collective-permute-start(bf16[256,768]{1,0:T(8,128)(2,1)} %get-tuple-element.181), channel_id=1, source_target_pairs={{0,0},{1,1},{2,4},{3,5},{4,2},{5,3},{6,6},{7,7},{8,8},{9,9},{10,12... | collective-permute-start | bytes 1179656 | tf_op jit(solution)/shard_map/ppermute | solution.py:107
  7.4 15.8 %collective-permute-start.1 = (bf16[256,768]{1,0:T(8,128)(2,1)}, bf16[256,768]{1,0:T(8,128)(2,1)}, u32[]{:S(2)}, u32[]{:S(2)}) collective-permute-start(bf16[256,768]{1,0:T(8,128)(2,1)} %get-tuple-element.182), channel_id=1, source_target_pairs={{0,1},{1,0},{2,5},{3,4},{4,3},{5,2},{6,7},{7,6},{8,9},{9,8},{10,13... | collective-permute-start | bytes 1179656 | tf_op jit(solution)/shard_map/ppermute | solution.py:108
  10.4 4.4 collective-permute-start.2
  11.0 9.1 %collective-permute-start.3 = (s32[256]{0:T(256)}, s32[256]{0:T(256)}, u32[]{:S(2)}, u32[]{:S(2)}) collective-permute-start(s32[256]{0:T(256)} %bitcast.20), channel_id=1, source_target_pairs={{0,0},{1,1},{2,4},{3,5},{4,2},{5,3},{6,6},{7,7},{8,8},{9,9},{10,12... | collective-permute-start | bytes 3080 | tf_op jit(solution)/shard_map/ppermute | solution.py:107
  12.9 8.0 %collective-permute-start.4 = (s32[256]{0:T(256)}, s32[256]{0:T(256)}, u32[]{:S(2)}, u32[]{:S(2)}) collective-permute-start(s32[256]{0:T(256)} %bitcast.21), channel_id=1, source_target_pairs={{0,1},{1,0},{2,5},{3,4},{4,3},{5,2},{6,7},{7,6},{8,9},{9,8},{10,13... | collective-permute-start | bytes 3080 | tf_op jit(solution)/shard_map/ppermute | solution.py:108
  17.3 8.7 %copy-start.45 = (f32[768]{0:T(1024)S(1)}, f32[768]{0:T(1024)}, u32[]{:S(2)}) copy-start(f32[768]{0:T(1024)} %convert_element_type.397) | copy-start | bytes 9220
  20.1 9.3 %copy-start.39 = (f32[768]{0:T(1024)}, f32[768]{0:T(1024)S(1)}, u32[]{:S(2)}) copy-start(f32[768]{0:T(1024)S(1)} %get-tuple-element.215) | copy-start | bytes 9220
  20.1 9.3 %copy-start.41 = (f32[768]{0:T(1024)}, f32[768]{0:T(1024)S(1)}, u32[]{:S(2)}) copy-start(f32[768]{0:T(1024)S(1)} %get-tuple-element.216) | copy-start | bytes 9220
  44.3 9.1 %copy-start.19 = (bf16[2,256,768]{2,1,0:T(8,128)(2,1)S(1)}, bf16[2,256,768]{2,1,0:T(8,128)(2,1)}, u32[]{:S(2)}) copy-start(bf16[2,256,768]{2,1,0:T(8,128)(2,1)} %param.27) | copy-start | bytes 2359300
  47.0 21.0 %collective-permute-start.5 = (bf16[512,1536]{1,0:T(8,128)(2,1)}, bf16[512,1536]{1,0:T(8,128)(2,1)}, u32[]{:S(2)}, u32[]{:S(2)}) collective-permute-start(bf16[512,1536]{1,0:T(8,128)(2,1)} %pad_maximum_fusion.3), channel_id=1, source_target_pairs={{0,4},{1,5},{2,6},{3,7},{4,0},{5,1},{6,2},{7,3},{8,12},{9,13},{10,... | collective-permute-start | bytes 4718600 | tf_op jit(solution)/shard_map/ppermute | solution.py:169
  54.4 62.3 %collective-permute-start.8 = (bf16[256,768]{1,0:T(8,128)(2,1)}, bf16[256,768]{1,0:T(8,128)(2,1)}, u32[]{:S(2)}, u32[]{:S(2)}) collective-permute-start(bf16[256,768]{1,0:T(8,128)(2,1)} %get-tuple-element.175), channel_id=1, source_target_pairs={{0,0},{1,1},{2,4},{3,5},{4,2},{5,3},{6,6},{7,7},{8,8},{9,9},{10,12... | collective-permute-start | bytes 1179656 | tf_op jit(solution)/shard_map/ppermute | solution.py:107
  59.1 57.6 %collective-permute-start.9 = (bf16[256,768]{1,0:T(8,128)(2,1)}, bf16[256,768]{1,0:T(8,128)(2,1)}, u32[]{:S(2)}, u32[]{:S(2)}) collective-permute-start(bf16[256,768]{1,0:T(8,128)(2,1)} %get-tuple-element.176), channel_id=1, source_target_pairs={{0,1},{1,0},{2,5},{3,4},{4,3},{5,2},{6,7},{7,6},{8,9},{9,8},{10,13... | collective-permute-start | bytes 1179656 | tf_op jit(solution)/shard_map/ppermute | solution.py:108
  111.8 17.8 %slice-start.2 = ((s8[4718592]{0:T(1024)(128)(4,1)}), s8[4194304]{0:T(1024)(128)(4,1)S(1)}, s32[]{:S(2)}) async-start(s8[4718592]{0:T(1024)(128)(4,1)} %bitcast.309), calls=%async_computation.2 | async-start | bytes 8388608
  116.7 12.9 %slice-start.3 = ((s8[4718592]{0:T(1024)(128)(4,1)}), s8[524288]{0:T(1024)(128)(4,1)S(1)}, s32[]{:S(2)}) async-start(s8[4718592]{0:T(1024)(128)(4,1)} %bitcast.309), calls=%async_computation.3 | async-start | bytes 1048576
  124.6 8.7 %slice-start.4 = ((s8[4718592]{0:T(1024)(128)(4,1)}), s8[4194304]{0:T(1024)(128)(4,1)S(1)}, s32[]{:S(2)}) async-start(s8[4718592]{0:T(1024)(128)(4,1)} %bitcast.311), calls=%async_computation.4 | async-start | bytes 8388608
  188.8 238.0 %collective-permute-start.33 = (bf16[2,2,4,576,128]{4,3,2,1,0:T(8,128)(2,1)}, bf16[2,2,4,576,128]{4,3,2,1,0:T(8,128)(2,1)}, u32[]{:S(2)}, u32[]{:S(2)}) collective-permute-start(bf16[2,2,4,576,128]{4,3,2,1,0:T(8,128)(2,1)} %dynamic-slice_bitcast_fusion.1), channel_id=1, source_target_pairs={{0,4},{1,5},{2,6},{3,7},{4,0},{5,1},{6,2},{7,3},{8,12},{9,13},{10,... | collective-permute-start | bytes 7077896 | tf_op jit(solution)/shard_map/ppermute | solution.py:125
  216.8 220.1 %collective-permute-start.28 = (bf16[2,2,4,576,128]{4,3,2,1,0:T(8,128)(2,1)}, bf16[2,2,4,576,128]{4,3,2,1,0:T(8,128)(2,1)}, u32[]{:S(2)}, u32[]{:S(2)}) collective-permute-start(bf16[2,2,4,576,128]{4,3,2,1,0:T(8,128)(2,1)} %dynamic-slice_bitcast_fusion.2), channel_id=1, source_target_pairs={{0,4},{1,5},{2,6},{3,7},{4,0},{5,1},{6,2},{7,3},{8,12},{9,13},{10,... | collective-permute-start | bytes 7077896 | tf_op jit(solution)/shard_map/ppermute | solution.py:125
  230.5 61.6 %collective-permute-start.23 = (bf16[2,2,4,144,128]{4,3,2,1,0:T(8,128)(2,1)}, bf16[2,2,4,144,128]{4,3,2,1,0:T(8,128)(2,1)}, u32[]{:S(2)}, u32[]{:S(2)}) collective-permute-start(bf16[2,2,4,144,128]{4,3,2,1,0:T(8,128)(2,1)} %dynamic-slice_bitcast_fusion.10), channel_id=1, source_target_pairs={{0,4},{1,5},{2,6},{3,7},{4,0},{5,1},{6,2},{7,3},{8,12},{9,13},{10,... | collective-permute-start | bytes 1769480 | tf_op jit(solution)/shard_map/ppermute | solution.py:125
  293.6 9.2 %collective-permute-start.24 = (bf16[2,4,144,128]{3,2,1,0:T(8,128)(2,1)S(1)}, bf16[2,4,144,128]{3,2,1,0:T(8,128)(2,1)S(1)}, u32[]{:S(2)}, u32[]{:S(2)}) collective-permute-start(bf16[2,4,144,128]{3,2,1,0:T(8,128)(2,1)S(1)} %dynamic-slice_bitcast_fusion.17), channel_id=1, source_target_pairs={{0,8},{1,9},{2,10},{3,11},{4,12},{5,13},{6,14},{7,15},{8,0},{9,1},... | collective-permute-start | bytes 884744 | tf_op jit(solution)/shard_map/ppermute | solution.py:125
  297.7 8.8 %copy-start.10 = (bf16[4,3,512,64]{2,3,1,0:T(8,128)(2,1)S(1)}, bf16[4,3,512,64]{2,3,1,0:T(8,128)(2,1)}, u32[]{:S(2)}) copy-start(bf16[4,3,512,64]{2,3,1,0:T(8,128)(2,1)} %get-tuple-element.94) | copy-start | bytes 2359300
  297.7 38.5 %collective-permute-start.10 = (bf16[512,1536]{0,1:T(8,128)(2,1)}, bf16[512,1536]{0,1:T(8,128)(2,1)}, u32[]{:S(2)}, u32[]{:S(2)}) collective-permute-start(bf16[512,1536]{0,1:T(8,128)(2,1)} %pad_maximum_fusion.2), channel_id=1, source_target_pairs={{0,4},{1,5},{2,6},{3,7},{4,0},{5,1},{6,2},{7,3},{8,12},{9,13},{10,... | collective-permute-start | bytes 4718600 | tf_op jit(solution)/shard_map/ppermute | solution.py:240
  304.3 6.1 %collective-permute-start.25 = (bf16[4,144,128]{2,1,0:T(8,128)(2,1)}, bf16[4,144,128]{2,1,0:T(8,128)(2,1)}, u32[]{:S(2)}, u32[]{:S(2)}) collective-permute-start(bf16[4,144,128]{2,1,0:T(8,128)(2,1)} %dynamic-slice_bitcast_fusion.19), channel_id=1, source_target_pairs={{0,16},{1,17},{2,18},{3,19},{4,20},{5,21},{6,22},{7,23},{8,24},{9,... | collective-permute-start | bytes 442376 | tf_op jit(solution)/shard_map/ppermute | solution.py:125
  306.5 34.5 %copy-start.35 = (f32[768]{0:T(1024)}, f32[768]{0:T(1024)S(1)}, u32[]{:S(2)}) copy-start(f32[768]{0:T(1024)S(1)} %get-tuple-element.210) | copy-start | bytes 9220
  308.6 4.2 collective-permute-start.6
  310.5 11.3 %collective-permute-start.7 = (bf16[256,768]{1,0:T(8,128)(2,1)}, bf16[256,768]{1,0:T(8,128)(2,1)S(1)}, u32[]{:S(2)}, u32[]{:S(2)}) collective-permute-start(bf16[256,768]{1,0:T(8,128)(2,1)} %get-tuple-element.180), channel_id=1, source_target_pairs={{1,0},{0,1},{5,2},{4,3},{3,4},{2,5},{7,6},{6,7},{9,8},{8,9},{13,10... | collective-permute-start | bytes 1179656 | tf_op jit(solution)/shard_map/ppermute | solution.py:113
  312.8 10.5 %collective-permute-start.26 = (bf16[2,144,128]{2,1,0:T(8,128)(2,1)S(1)}, bf16[2,144,128]{2,1,0:T(8,128)(2,1)S(1)}, u32[]{:S(2)}, u32[]{:S(2)}) collective-permute-start(bf16[2,144,128]{2,1,0:T(8,128)(2,1)S(1)} %pad_maximum_fusion.18), channel_id=1, source_target_pairs={{0,1},{1,0},{2,3},{3,2},{4,5},{5,4},{6,7},{7,6},{8,9},{9,8},{10,11... | collective-permute-start | bytes 221192 | tf_op jit(solution)/shard_map/ppermute | solution.py:131
  323.4 10.6 %collective-permute-start.27 = (bf16[144,128]{1,0:T(8,128)(2,1)S(1)}, bf16[144,128]{1,0:T(8,128)(2,1)S(1)}, u32[]{:S(2)}, u32[]{:S(2)}) collective-permute-start(bf16[144,128]{1,0:T(8,128)(2,1)S(1)} %fusion.114), channel_id=1, source_target_pairs={{0,3},{1,2},{2,1},{3,0},{4,7},{5,6},{6,5},{7,4},{8,11},{9,10},{10,... | collective-permute-start | bytes 110600 | tf_op jit(solution)/shard_map/ppermute | solution.py:133
  341.6 9.4 %copy-start.48 = (f32[768]{0:T(1024)S(1)}, f32[768]{0:T(1024)}, u32[]{:S(2)}) copy-start(f32[768]{0:T(1024)} %get-tuple-element.113) | copy-start | bytes 9220
  341.6 10.7 %copy-start.32 = (bf16[768]{0:T(1024)(128)(2,1)S(1)}, bf16[768]{0:T(1024)(128)(2,1)}, u32[]{:S(2)}) copy-start(bf16[768]{0:T(1024)(128)(2,1)} %param.24) | copy-start | bytes 4612
  341.6 12.0 %copy-start.49 = (f32[768]{0:T(1024)S(1)}, f32[768]{0:T(1024)}, u32[]{:S(2)}) copy-start(f32[768]{0:T(1024)} %get-tuple-element.165) | copy-start | bytes 9220
  379.0 44.5 %collective-permute-start.13 = (bf16[2,2,4,22720]{3,2,1,0:T(4,128)(2,1)}, bf16[2,2,4,22720]{3,2,1,0:T(4,128)(2,1)}, u32[]{:S(2)}, u32[]{:S(2)}) collective-permute-start(bf16[2,2,4,22720]{3,2,1,0:T(4,128)(2,1)} %dynamic-slice_bitcast_fusion.7), channel_id=1, source_target_pairs={{0,4},{1,5},{2,6},{3,7},{4,0},{5,1},{6,2},{7,3},{8,12},{9,13},{10,... | collective-permute-start | bytes 2181128 | tf_op jit(solution)/shard_map/ppermute | solution.py:125
  380.5 10.7 %copy-start.21 = (bf16[512,768]{0,1:T(8,128)(2,1)S(1)}, bf16[512,768]{0,1:T(8,128)(2,1)}, u32[]{:S(2)}) copy-start(bf16[512,768]{0,1:T(8,128)(2,1)} %copy-done.20) | copy-start | bytes 2359300
  380.5 10.7 %copy-start.38 = (f32[512]{0:T(512)S(1)}, f32[512]{0:T(512)}, u32[]{:S(2)}) copy-start(f32[512]{0:T(512)} %copy-done.36) | copy-start | bytes 6148
  380.5 10.7 %copy-start.40 = (f32[768]{0:T(1024)S(1)}, f32[768]{0:T(1024)}, u32[]{:S(2)}) copy-start(f32[768]{0:T(1024)} %copy-done.39) | copy-start | bytes 9220
  380.5 10.7 %copy-start.42 = (f32[768]{0:T(1024)S(1)}, f32[768]{0:T(1024)}, u32[]{:S(2)}) copy-start(f32[768]{0:T(1024)} %copy-done.41) | copy-start | bytes 9220
  380.5 10.7 %copy-start.46 = (f32[768]{0:T(1024)S(1)}, f32[768]{0:T(1024)}, u32[]{:S(2)}) copy-start(f32[768]{0:T(1024)} %convert_element_type.397) | copy-start | bytes 9220
  384.2 37.0 %collective-permute-start.11 = (bf16[256,768]{1,0:T(8,128)(2,1)}, bf16[256,768]{1,0:T(8,128)(2,1)}, u32[]{:S(2)}, u32[]{:S(2)}) collective-permute-start(bf16[256,768]{1,0:T(8,128)(2,1)} %get-tuple-element.173), channel_id=1, source_target_pairs={{0,0},{1,1},{4,2},{5,3},{2,4},{3,5},{6,6},{7,7},{8,8},{9,9},{12,10... | collective-permute-start | bytes 1179656 | tf_op jit(solution)/shard_map/ppermute | solution.py:112
  388.7 32.6 %collective-permute-start.12 = (bf16[256,768]{1,0:T(8,128)(2,1)}, bf16[256,768]{1,0:T(8,128)(2,1)}, u32[]{:S(2)}, u32[]{:S(2)}) collective-permute-start(bf16[256,768]{1,0:T(8,128)(2,1)} %get-tuple-element.174), channel_id=1, source_target_pairs={{1,0},{0,1},{5,2},{4,3},{3,4},{2,5},{7,6},{6,7},{9,8},{8,9},{13,10... | collective-permute-start | bytes 1179656 | tf_op jit(solution)/shard_map/ppermute | solution.py:113
  421.2 62.4 %collective-permute-start.18 = (bf16[2,2,4,432,128]{4,3,2,1,0:T(8,128)(2,1)}, bf16[2,2,4,432,128]{4,3,2,1,0:T(8,128)(2,1)}, u32[]{:S(2)}, u32[]{:S(2)}) collective-permute-start(bf16[2,2,4,432,128]{4,3,2,1,0:T(8,128)(2,1)} %dynamic-slice_bitcast_fusion.3), channel_id=1, source_target_pairs={{0,4},{1,5},{2,6},{3,7},{4,0},{5,1},{6,2},{7,3},{8,12},{9,13},{10,... | collective-permute-start | bytes 5308424 | tf_op jit(solution)/shard_map/ppermute | solution.py:125
  425.0 11.9 %slice-start = ((s8[4718592]{0:T(1024)(128)(4,1)}), s8[4194304]{0:T(1024)(128)(4,1)S(1)}, s32[]{:S(2)}) async-start(s8[4718592]{0:T(1024)(128)(4,1)} %bitcast.288), calls=%async_computation | async-start | bytes 8388608
  425.2 11.7 %slice-start.1 = ((s8[4718592]{0:T(1024)(128)(4,1)}), s8[524288]{0:T(1024)(128)(4,1)S(1)}, s32[]{:S(2)}) async-start(s8[4718592]{0:T(1024)(128)(4,1)} %bitcast.288), calls=%async_computation.1 | async-start | bytes 1048576
  425.2 10.8 %collective-permute-start.14 = (bf16[2,4,22720]{2,1,0:T(4,128)(2,1)S(1)}, bf16[2,4,22720]{2,1,0:T(4,128)(2,1)S(1)}, u32[]{:S(2)}, u32[]{:S(2)}) collective-permute-start(bf16[2,4,22720]{2,1,0:T(4,128)(2,1)S(1)} %dynamic-slice_bitcast_fusion.16), channel_id=1, source_target_pairs={{0,8},{1,9},{2,10},{3,11},{4,12},{5,13},{6,14},{7,15},{8,0},{9,1},... | collective-permute-start | bytes 1090568 | tf_op jit(solution)/shard_map/ppermute | solution.py:125
  431.0 49.7 %collective-permute-start.34 = (bf16[2,4,576,128]{3,2,1,0:T(8,128)(2,1)}, bf16[2,4,576,128]{3,2,1,0:T(8,128)(2,1)}, u32[]{:S(2)}, u32[]{:S(2)}) collective-permute-start(bf16[2,4,576,128]{3,2,1,0:T(8,128)(2,1)} %dynamic-slice_bitcast_fusion.4), channel_id=1, source_target_pairs={{0,16},{1,17},{2,18},{3,19},{4,20},{5,21},{6,22},{7,23},{8,24},{9,... | collective-permute-start | bytes 3538952 | tf_op jit(solution)/shard_map/ppermute | solution.py:125
  436.3 26.7 %collective-permute-start.15 = (bf16[4,22720]{1,0:T(4,128)(2,1)S(1)}, bf16[4,22720]{1,0:T(4,128)(2,1)S(1)}, u32[]{:S(2)}, u32[]{:S(2)}) collective-permute-start(bf16[4,22720]{1,0:T(4,128)(2,1)S(1)} %dynamic-slice_bitcast_fusion.18), channel_id=1, source_target_pairs={{0,16},{1,17},{2,18},{3,19},{4,20},{5,21},{6,22},{7,23},{8,24},{9,... | collective-permute-start | bytes 545288 | tf_op jit(solution)/shard_map/ppermute | solution.py:125
  439.2 25.8 %copy-start.4 = (bf16[2,2,4,576,128]{4,3,2,1,0:T(8,128)(2,1)}, bf16[2,2,4,576,128]{4,3,2,1,0:T(8,128)(2,1)S(1)}, u32[]{:S(2)}) copy-start(bf16[2,2,4,576,128]{4,3,2,1,0:T(8,128)(2,1)S(1)} %fusion.65) | copy-start | bytes 7077892
  463.7 4.6 collective-permute-start.16
  465.0 29.2 %collective-permute-start.29 = (bf16[2,4,576,128]{3,2,1,0:T(8,128)(2,1)}, bf16[2,4,576,128]{3,2,1,0:T(8,128)(2,1)}, u32[]{:S(2)}, u32[]{:S(2)}) collective-permute-start(bf16[2,4,576,128]{3,2,1,0:T(8,128)(2,1)} %dynamic-slice_bitcast_fusion.5), channel_id=1, source_target_pairs={{0,8},{1,9},{2,10},{3,11},{4,12},{5,13},{6,14},{7,15},{8,0},{9,1},... | collective-permute-start | bytes 3538952 | tf_op jit(solution)/shard_map/ppermute | solution.py:125
  468.9 5.9 %collective-permute-start.17 = (bf16[22720]{0:T(1024)(128)(2,1)S(1)}, bf16[22720]{0:T(1024)(128)(2,1)S(1)}, u32[]{:S(2)}, u32[]{:S(2)}) collective-permute-start(bf16[22720]{0:T(1024)(128)(2,1)S(1)} %fusion.112), channel_id=1, source_target_pairs={{0,3},{1,2},{2,1},{3,0},{4,7},{5,6},{6,5},{7,4},{8,11},{9,10},{10,... | collective-permute-start | bytes 136328 | tf_op jit(solution)/shard_map/ppermute | solution.py:133
  482.8 11.4 %copy-start.5 = (bf16[2,2,4,576,128]{4,3,2,1,0:T(8,128)(2,1)S(1)}, bf16[2,2,4,576,128]{4,3,2,1,0:T(8,128)(2,1)}, u32[]{:S(2)}) copy-start(bf16[2,2,4,576,128]{4,3,2,1,0:T(8,128)(2,1)} %copy-done.4) | copy-start | bytes 7077892
  482.8 22.1 %collective-permute-start.35 = (bf16[4,576,128]{2,1,0:T(8,128)(2,1)S(1)}, bf16[4,576,128]{2,1,0:T(8,128)(2,1)S(1)}, u32[]{:S(2)}, u32[]{:S(2)}) collective-permute-start(bf16[4,576,128]{2,1,0:T(8,128)(2,1)S(1)} %dynamic-slice_bitcast_fusion.8), channel_id=1, source_target_pairs={{0,8},{1,9},{2,10},{3,11},{4,12},{5,13},{6,14},{7,15},{8,0},{9,1},... | collective-permute-start | bytes 1769480 | tf_op jit(solution)/shard_map/ppermute | solution.py:125
  495.9 16.3 %collective-permute-start.30 = (bf16[4,576,128]{2,1,0:T(8,128)(2,1)S(1)}, bf16[4,576,128]{2,1,0:T(8,128)(2,1)S(1)}, u32[]{:S(2)}, u32[]{:S(2)}) collective-permute-start(bf16[4,576,128]{2,1,0:T(8,128)(2,1)S(1)} %dynamic-slice_bitcast_fusion.9), channel_id=1, source_target_pairs={{0,16},{1,17},{2,18},{3,19},{4,20},{5,21},{6,22},{7,23},{8,24},{9,... | collective-permute-start | bytes 1769480 | tf_op jit(solution)/shard_map/ppermute | solution.py:125
  496.5 30.1 %collective-permute-start.19 = (bf16[2,4,432,128]{3,2,1,0:T(8,128)(2,1)S(1)}, bf16[2,4,432,128]{3,2,1,0:T(8,128)(2,1)S(1)}, u32[]{:S(2)}, u32[]{:S(2)}) collective-permute-start(bf16[2,4,432,128]{3,2,1,0:T(8,128)(2,1)S(1)} %dynamic-slice_bitcast_fusion.6), channel_id=1, source_target_pairs={{0,16},{1,17},{2,18},{3,19},{4,20},{5,21},{6,22},{7,23},{8,24},{9,... | collective-permute-start | bytes 2654216 | tf_op jit(solution)/shard_map/ppermute | solution.py:125
  505.2 22.2 %collective-permute-start.36 = (bf16[2,576,128]{2,1,0:T(8,128)(2,1)S(1)}, bf16[2,576,128]{2,1,0:T(8,128)(2,1)S(1)}, u32[]{:S(2)}, u32[]{:S(2)}) collective-permute-start(bf16[2,576,128]{2,1,0:T(8,128)(2,1)S(1)} %pad_maximum_fusion.15), channel_id=1, source_target_pairs={{0,1},{1,0},{2,3},{3,2},{4,5},{5,4},{6,7},{7,6},{8,9},{9,8},{10,11... | collective-permute-start | bytes 884744 | tf_op jit(solution)/shard_map/ppermute | solution.py:131
  512.5 17.1 %collective-permute-start.31 = (bf16[2,576,128]{2,1,0:T(8,128)(2,1)S(1)}, bf16[2,576,128]{2,1,0:T(8,128)(2,1)S(1)}, u32[]{:S(2)}, u32[]{:S(2)}) collective-permute-start(bf16[2,576,128]{2,1,0:T(8,128)(2,1)S(1)} %pad_maximum_fusion.14), channel_id=1, source_target_pairs={{0,1},{1,0},{2,3},{3,2},{4,5},{5,4},{6,7},{7,6},{8,9},{9,8},{10,11... | collective-permute-start | bytes 884744 | tf_op jit(solution)/shard_map/ppermute | solution.py:131
  526.9 8.4 %collective-permute-start.20 = (bf16[4,432,128]{2,1,0:T(8,128)(2,1)S(1)}, bf16[4,432,128]{2,1,0:T(8,128)(2,1)S(1)}, u32[]{:S(2)}, u32[]{:S(2)}) collective-permute-start(bf16[4,432,128]{2,1,0:T(8,128)(2,1)S(1)} %dynamic-slice_bitcast_fusion.11), channel_id=1, source_target_pairs={{0,8},{1,9},{2,10},{3,11},{4,12},{5,13},{6,14},{7,15},{8,0},{9,1},... | collective-permute-start | bytes 1327112 | tf_op jit(solution)/shard_map/ppermute | solution.py:125
  527.5 9.5 %collective-permute-start.37 = (bf16[576,128]{1,0:T(8,128)(2,1)S(1)}, bf16[576,128]{1,0:T(8,128)(2,1)S(1)}, u32[]{:S(2)}, u32[]{:S(2)}) collective-permute-start(bf16[576,128]{1,0:T(8,128)(2,1)S(1)} %fusion.110), channel_id=1, source_target_pairs={{0,3},{1,2},{2,1},{3,0},{4,7},{5,6},{6,5},{7,4},{8,11},{9,10},{10,... | collective-permute-start | bytes 442376 | tf_op jit(solution)/shard_map/ppermute | solution.py:133
  529.6 15.3 %collective-permute-start.32 = (bf16[576,128]{1,0:T(8,128)(2,1)S(1)}, bf16[576,128]{1,0:T(8,128)(2,1)S(1)}, u32[]{:S(2)}, u32[]{:S(2)}) collective-permute-start(bf16[576,128]{1,0:T(8,128)(2,1)S(1)} %fusion.109), channel_id=1, source_target_pairs={{0,3},{1,2},{2,1},{3,0},{4,7},{5,6},{6,5},{7,4},{8,11},{9,10},{10,... | collective-permute-start | bytes 442376 | tf_op jit(solution)/shard_map/ppermute | solution.py:133
  535.5 6.0 %collective-permute-start.21 = (bf16[2,432,128]{2,1,0:T(8,128)(2,1)S(1)}, bf16[2,432,128]{2,1,0:T(8,128)(2,1)S(1)}, u32[]{:S(2)}, u32[]{:S(2)}) collective-permute-start(bf16[2,432,128]{2,1,0:T(8,128)(2,1)S(1)} %pad_maximum_fusion.16), channel_id=1, source_target_pairs={{0,1},{1,0},{2,3},{3,2},{4,5},{5,4},{6,7},{7,6},{8,9},{9,8},{10,11... | collective-permute-start | bytes 663560 | tf_op jit(solution)/shard_map/ppermute | solution.py:131
  543.0 8.1 %collective-permute-start.22 = (bf16[432,128]{1,0:T(8,128)(2,1)}, bf16[432,128]{1,0:T(8,128)(2,1)}, u32[]{:S(2)}, u32[]{:S(2)}) collective-permute-start(bf16[432,128]{1,0:T(8,128)(2,1)} %fusion.111), channel_id=1, source_target_pairs={{0,3},{1,2},{2,1},{3,0},{4,7},{5,6},{6,5},{7,4},{8,11},{9,10},{10,... | collective-permute-start | bytes 331784 | tf_op jit(solution)/shard_map/ppermute | solution.py:133
  (36 other events, 119.5 us)
